TPU v7x, 32 devices: a whole 2x2x4 slice. The times are simulated.
32 devices in a mesh: clip: 2 (over y), tm: 4 (over x, core), mp: 4 (over z).
Axes of the slice: x: 2, y: 2, z: 4, core: 2. Of those that a mesh axis runs over, the one named last changes fastest.
Arguments:
- token_ids: int32 [8, 256], P(('clip', 'tm')), parts along dimension 0, may hold values from 0 to 1023
- remask: int32 [8, 256], P(('clip', 'tm')), parts along dimension 0, may hold values from -1 to 255, as said below
- position_embed: bfloat16 [4, 256, 1024], P('tm'), may hold values from -0.625 to 0.625
- mask_embed: bfloat16 [1024], replicated, may hold values from -0.625 to 0.625
- table: bfloat16 [1024, 1024], P('mp')
- gain_in: float32 [1024], replicated, may hold values from 0.5 to 1.5
- gain_out: float32 [1024], replicated, may hold values from 0.5 to 1.5
- w_qkv: bfloat16 [3, 1024, 1024], P(None, None, 'mp')
- w_out: bfloat16 [1024, 1024], P('mp'), may hold values from -0.1875 to 0.1875
Outputs:
- log_probs: bfloat16 [8, 256, 1024], P(('clip', 'tm'), None, 'mp'), parts along dimension 0
- confidence: float32 [8, 256], P(('clip', 'tm')), parts along dimension 0
- clip_stats: float32 [4], P('clip'), parts along dimension 0
There are 2 independent parts, one for each index of `clip`. A program takes and returns all parts, laid end to end along the dimension named above; an argument that names none is the same for every part. Nothing has to cross between parts.
Inputs may be any that keep to these rules, and one draw needn't show every extreme that they name: `remask`: row f lists distinct masked positions of frame f in its first slots and -1 in the unused ones; every frame lists at least one position.
All inputs are finite; a program needn't handle non-finite values.
Results may differ from a plain program's by a relative error of at most 0.019.
The roundings to bfloat16 on the way count: a program that leaves them out, or rounds other values in their place, can miss the bound.
Values may be sent and summed in bfloat16 or wider, within the bound.
No kernel may reach another device: no remote copies, remote signals or barrier semaphores. Data moves between devices by JAX's collectives and lax.ppermute only.
A program may use at most 64 MiB of HBM per device.

v0:
```python
import math

import jax
import jax.numpy as jnp
from jax import lax
from jax.sharding import PartitionSpec as P

HEAD_DIM = 64


def layer_norm(values, gain):
    center = values - jnp.mean(values, axis=-1, keepdims=True)
    spread = jnp.mean(center * center, axis=-1, keepdims=True)
    return center * lax.rsqrt(spread + 1e-05) * gain


def absorb_block(state, query, key_block, value_block):
    running, totals, summed = state
    scores = jnp.einsum(
        "qhd,khd->hqk", query, key_block, preferred_element_type=jnp.float32
    ) * HEAD_DIM ** (-0.5)
    raised = jnp.maximum(running, jnp.max(scores, axis=-1))
    fade = jnp.exp(running - raised)
    weights = jnp.exp(scores - raised[:, :, None])
    totals = totals * fade + jnp.sum(weights, axis=-1)
    summed = summed * fade[:, :, None] + jnp.einsum(
        "hqk,khd->hqd",
        weights.astype(jnp.bfloat16),
        value_block,
        preferred_element_type=jnp.float32,
    )
    return (raised, totals, summed)


def sweep_keys(state, query, key_rows, value_rows):
    count = key_rows.shape[0]
    block = math.gcd(count, 512)
    heads_here = query.shape[1]
    key_blocks = key_rows.reshape(count // block, block, heads_here, HEAD_DIM)
    value_blocks = value_rows.reshape(count // block, block, heads_here, HEAD_DIM)

    def advance(inner, pair):
        return (absorb_block(inner, query, pair[0], pair[1]), None)

    state, ignored = lax.scan(advance, state, (key_blocks, value_blocks))
    return state


def empty_state(heads_here, row_count):
    return (
        jnp.full((heads_here, row_count), -1e30, jnp.float32),
        jnp.zeros((heads_here, row_count), jnp.float32),
        jnp.zeros((heads_here, row_count, HEAD_DIM), jnp.float32),
    )


def body(token_ids, remask, position_embed, mask_embed, table, gain_in, gain_out, w_qkv, w_out):
    frames_here, frame_span = token_ids.shape
    row_count = frames_here * frame_span
    parts_mp = lax.axis_size("mp")
    vocab_here = table.shape[0]
    local_width = w_qkv.shape[2]
    heads_here = local_width // HEAD_DIM
    offset = lax.axis_index("mp") * vocab_here
    spots = jnp.arange(frame_span, dtype=jnp.int32)
    masked = jnp.any(remask[:, None, :] == spots[None, :, None], axis=-1).reshape(row_count)
    flat_ids = token_ids.reshape(row_count)
    entries = offset + jnp.arange(vocab_here, dtype=jnp.int32)
    onehot = ((flat_ids[:, None] == entries[None, :]) & jnp.logical_not(masked)[:, None]).astype(
        jnp.bfloat16
    )
    added_rows = jnp.where(masked[:, None], mask_embed.astype(jnp.float32)[None, :], 0.0)
    added_rows = added_rows + position_embed.reshape(row_count, -1).astype(jnp.float32)
    share = row_count // parts_mp
    first_row = lax.axis_index("mp") * share
    looked = lax.psum_scatter(
        jnp.dot(onehot, table, preferred_element_type=jnp.float32).astype(jnp.bfloat16),
        "mp",
        scatter_dimension=0,
        tiled=True,
    ).astype(jnp.float32)
    hidden_in = looked + lax.dynamic_slice_in_dim(added_rows, first_row, share, 0)
    normed = layer_norm(hidden_in, gain_in).astype(jnp.bfloat16)
    projected = jnp.einsum(
        "rd,jdc->jrc",
        lax.all_gather(normed, "mp", axis=0, tiled=True),
        w_qkv,
        preferred_element_type=jnp.float32,
    ).astype(jnp.bfloat16)
    query = projected[0].reshape(row_count, heads_here, HEAD_DIM)
    keys = projected[1]
    values = projected[2]
    highest, totals, summed = sweep_keys(
        empty_state(heads_here, row_count),
        query,
        lax.all_gather(keys, "tm", axis=0, tiled=True),
        lax.all_gather(values, "tm", axis=0, tiled=True),
    )
    context = (
        (summed / totals[:, :, None])
        .transpose(1, 0, 2)
        .reshape(row_count, local_width)
        .astype(jnp.bfloat16)
    )
    mixed_rows = lax.psum_scatter(
        jnp.dot(context, w_out, preferred_element_type=jnp.float32),
        "mp",
        scatter_dimension=0,
        tiled=True,
    )
    final_local = layer_norm(hidden_in + mixed_rows, gain_out).astype(jnp.bfloat16)
    logits = lax.dot_general(
        lax.all_gather(final_local, "mp", axis=0, tiled=True),
        table,
        (((1,), (1,)), ((), ())),
        preferred_element_type=jnp.float32,
    )
    local_max = jnp.max(logits, axis=-1)
    row_max = lax.pmax(local_max, "mp")
    row_total = lax.psum(jnp.sum(jnp.exp(logits - row_max[:, None]), axis=-1), "mp")
    log_total = row_max + jnp.log(row_total)
    log_probs = (
        (logits - log_total[:, None])
        .astype(jnp.bfloat16)
        .reshape(frames_here, frame_span, vocab_here)
    )
    confidence = jnp.exp(row_max - log_total)
    weight = masked.astype(jnp.float32)
    conf_sum, count = lax.psum((jnp.sum(confidence * weight), jnp.sum(weight)), "tm")
    tokens_all = row_count * lax.axis_size("tm")
    clip_stats = jnp.stack([conf_sum / count, jnp.log(count / tokens_all)])
    return (log_probs, confidence.reshape(frames_here, frame_span), clip_stats)


def solution(mesh):
    return jax.shard_map(
        body,
        mesh=mesh,
        in_specs=(
            P(("clip", "tm"), None),
            P(("clip", "tm"), None),
            P("tm", None, None),
            P(),
            P("mp", None),
            P(),
            P(),
            P(None, None, "mp"),
            P("mp", None),
        ),
        out_specs=(P(("clip", "tm"), None, "mp"), P(("clip", "tm"), None), P("clip")),
        check_vma=False,
    )
```

profile of v0, /device:TPU:0, one launch (start us, length us, event | category | flops | bytes accessed | tf_op | source)
XLA Modules:
  0.0 160.6 jit_solution(13981228685784389720)
XLA Ops:
  7.2 0.9 fusion.18
  8.2 2.2 %convolution_convert_fusion = bf16[256,1024]{1,0:T(8,128)(2,1)} fusion(bf16[256,1024]{1,0:T(8,128)(2,1)} %param.15, s32[256]{0:T(256)S(1)} %iota_add_fusion, s32[256]{0:T(256)} %bitcast.66, pred[256]{0:T(512)(128)(4,1)S(1)} %not.7), kind=kOutput, calls=%fused_computation.21 | convolution fusion | flops 134610944 | bytes 1050880 | tf_op jit(solution)/shard_map/dot_general | solution.py:77
  11.3 23.9 %reduce-scatter.3.cloned.1.call-done = bf16[64,1024]{1,0:T(8,128)(2,1)} async-done(((bf16[256,1024]{1,0:T(8,128)(2,1)}), bf16[64,1024]{1,0:T(8,128)(2,1)}) %reduce-scatter.3.cloned.1.call-update) | async-done | bytes 131088 | tf_op jit(solution)/shard_map/reduce_scatter | solution.py:76
  35.1 1.2 fusion.26
  36.3 1.2 multiply_reduce_fusion.1
  37.6 1.1 multiply_convert_fusion.1
  38.7 15.5 %all_gather.12 = bf16[256,1024]{1,0:T(8,128)(2,1)S(1)} all-gather(bf16[64,1024]{1,0:T(8,128)(2,1)S(1)} %multiply_convert_fusion.1), channel_id=1, replica_groups=mesh['clip'=2,'tm'=4,'mp'=4] {'mp'}, dimensions={0}, use_global_device_ids=true | all-gather | bytes 655360 | tf_op jit(solution)/shard_map/all_gather | solution.py:86
  54.2 0.7 fusion.15
  55.0 7.1 %all-gather = bf16[1,1024,256]{1,2,0:T(8,128)(2,1)S(1)} all-gather(bf16[1,256,256]{1,2,0:T(8,128)(2,1)S(1)} %get-tuple-element.114), channel_id=2, replica_groups=mesh['clip'=2,'tm'=4,'mp'=4] {'tm'}, dimensions={1}, use_global_device_ids=true | all-gather | bytes 655360 | tf_op jit(solution)/shard_map/all_gather | solution.py:96
  62.6 7.3 %all-gather.1 = bf16[1,1024,256]{1,2,0:T(8,128)(2,1)S(1)} all-gather(bf16[1,256,256]{1,2,0:T(8,128)(2,1)S(1)} %get-tuple-element.112), channel_id=3, replica_groups=mesh['clip'=2,'tm'=4,'mp'=4] {'tm'}, dimensions={1}, use_global_device_ids=true | all-gather | bytes 655360 | tf_op jit(solution)/shard_map/all_gather | solution.py:97
  70.3 9.2 %while.15 = (s32[]{:T(128)}, f32[4,256]{1,0:T(4,128)S(1)}, f32[4,256]{1,0:T(4,128)S(1)}, f32[4,256,64]{1,2,0:T(8,128)S(1)}, bf16[2,512,4,64]{1,3,2,0:T(8,128)(2,...) while((s32[]{:T(128)}, f32[4,256]{1,0:T(4,128)S(1)}, ...), condition=%wide.region_7.8_spmd.clone, body=%wide.region_4.7_spmd.clone.sunk | while | flops 138613760 | bytes 15925389 | solution.py:45
  70.3 1.8 %bitcast_reduce_fusion.2 = (f32[4,256]{1,0:T(4,128)S(1)}, f32[4,512,256]{2,1,0:T(8,128)}) fusion(bf16[256,4,64]{0,2,1:T(8,128)(2,1)S(1)} %get-tuple-element.192, bf16[2,512,4,64]{1,3,2,0:T(8,128)(2,1)S(1)} %get-tuple-element.191, s32[]{:T(128)} %get-tuple-element.178), kind=kOutput, calls=%fused_computation.1.clone.1 | convolution fusion | flops 68156416 | bytes 2494468 | tf_op jit(solution)/shard_map/while/body/eval_jaxpr/qhd,khd->hqk/dot_general | solution.py:19
  72.2 2.1 %fusion.47 = f32[4,256]{1,0:T(4,128)S(1)} fusion(f32[4,512,256]{2,1,0:T(8,128)} %get-tuple-element.166, f32[4,256]{1,0:T(4,128)S(1)} %select_maximum_fusion.2), kind=kLoop, calls=%fused_computation.4.clone.1 | loop fusion | flops 1571840 | bytes 2105344 | tf_op jit(solution)/shard_map/while/body/eval_jaxpr/reduce_sum | solution.py:25
  74.9 1.8 %bitcast_reduce_fusion.2 = (f32[4,256]{1,0:T(4,128)S(1)}, f32[4,512,256]{2,1,0:T(8,128)}) fusion(bf16[256,4,64]{0,2,1:T(8,128)(2,1)S(1)} %get-tuple-element.192, bf16[2,512,4,64]{1,3,2,0:T(8,128)(2,1)S(1)} %get-tuple-element.191, s32[]{:T(128)} %get-tuple-element.178), kind=kOutput, calls=%fused_computation.1.clone.1 | convolution fusion | flops 68156416 | bytes 2494468 | tf_op jit(solution)/shard_map/while/body/eval_jaxpr/qhd,khd->hqk/dot_general | solution.py:19
  76.8 2.1 %fusion.47 = f32[4,256]{1,0:T(4,128)S(1)} fusion(f32[4,512,256]{2,1,0:T(8,128)} %get-tuple-element.166, f32[4,256]{1,0:T(4,128)S(1)} %select_maximum_fusion.2), kind=kLoop, calls=%fused_computation.4.clone.1 | loop fusion | flops 1571840 | bytes 2105344 | tf_op jit(solution)/shard_map/while/body/eval_jaxpr/reduce_sum | solution.py:25
  79.6 1.3 fusion.31
  81.0 25.1 %reduce-scatter.5.cloned.1.call-done = f32[64,1024]{1,0:T(8,128)} async-done(((f32[256,1024]{1,0:T(8,128)}), f32[64,1024]{1,0:T(8,128)}) %reduce-scatter.5.cloned.1.call-update) | async-done | bytes 262160 | tf_op jit(solution)/shard_map/reduce_scatter | solution.py:105
  106.1 1.2 fusion.27
  107.7 16.0 %all_gather.15 = bf16[256,1024]{1,0:T(8,128)(2,1)S(1)} all-gather(bf16[64,1024]{1,0:T(8,128)(2,1)S(1)} %multiply_convert_fusion), channel_id=1, replica_groups=mesh['clip'=2,'tm'=4,'mp'=4] {'mp'}, dimensions={0}, use_global_device_ids=true | all-gather | bytes 655360 | tf_op jit(solution)/shard_map/all_gather | solution.py:113
  124.1 8.4 %pmax.7 = f32[256]{0:T(256)S(1)} all-reduce(f32[256]{0:T(256)S(1)} %get-tuple-element.116), channel_id=1, replica_groups=mesh['clip'=2,'tm'=4,'mp'=4] {'mp'}, use_global_device_ids=true, to_apply=%region_12.13 | all-reduce | flops 256 | bytes 2048 | tf_op jit(solution)/shard_map/pmax | solution.py:119
  132.5 10.4 %psum.21 = f32[256]{0:T(256)S(1)} all-reduce(f32[256]{0:T(256)S(1)} %exponential_reduce_fusion), channel_id=1, replica_groups=mesh['clip'=2,'tm'=4,'mp'=4] {'mp'}, use_global_device_ids=true, to_apply=%region_14.15 | all-reduce | flops 256 | bytes 2048 | tf_op jit(solution)/shard_map/psum | solution.py:120
  142.9 1.2 select_reduce_fusion
  144.1 6.3 %all-reduce = (f32[]{:T(128)}, f32[]{:T(128)}) all-reduce(f32[]{:T(128)} %get-tuple-element.88, f32[]{:T(128)} %get-tuple-element.87), channel_id=1, replica_groups=mesh['clip'=2,'tm'=4,'mp'=4] {'tm'}, use_global_device_ids=true, to_apply=%region_18.19 | all-reduce | flops 2 | bytes 16 | tf_op jit(solution)/shard_map/psum | solution.py:129
  152.4 0.8 copy.21
  (59 shorter events, 4.5 us)
Async XLA Ops:
  7.2 47.0 %copy-start = (bf16[3,1024,256]{2,1,0:T(8,128)(2,1)S(1)}, bf16[3,1024,256]{2,1,0:T(8,128)(2,1)}, u32[]{:S(2)}) copy-start(bf16[3,1024,256]{2,1,0:T(8,128)(2,1)} %param.18) | copy-start | bytes 4718596
  7.2 30.4 %copy-start.7 = (f32[1024]{0:T(1024)S(1)}, f32[1024]{0:T(1024)}, u32[]{:S(2)}) copy-start(f32[1024]{0:T(1024)} %param.16) | copy-start | bytes 12292
  7.2 27.9 %reduce-scatter.3.cloned.1.call-start = ((), (), s32[]{:S(2)}) async-start(), calls=%async_computation.2 | async-start | bytes 655360 | tf_op jit(solution)/shard_map/reduce_scatter | solution.py:76
  8.1 27.0 %copy-start.9 = (pred[256]{0:T(512)(128)(4,1)}, pred[256]{0:T(512)(128)(4,1)S(1)}, u32[]{:S(2)}) copy-start(pred[256]{0:T(512)(128)(4,1)S(1)} %fusion.18) | copy-start | bytes 772
  10.4 95.7 %reduce-scatter.5.cloned.1.call-start = ((), (), s32[]{:S(2)}) async-start(), calls=%async_computation.3 | async-start | bytes 1310720 | tf_op jit(solution)/shard_map/reduce_scatter | solution.py:105
  10.6 44.4 %copy-start.5 = (pred[64]{0:T(512)(128)(4,1)}, pred[64]{0:T(512)(128)(4,1)S(1)}, u32[]{:S(2)}) copy-start(pred[64]{0:T(512)(128)(4,1)S(1)} %dynamic-slice) | copy-start | bytes 196
  70.3 9.3 %copy-start.4 = (bf16[256,1024]{1,0:T(8,128)(2,1)S(1)}, bf16[256,1024]{1,0:T(8,128)(2,1)}, u32[]{:S(2)}) copy-start(bf16[256,1024]{1,0:T(8,128)(2,1)} %param.19) | copy-start | bytes 1572868
  72.2 2.2 %copy-start.1 = (f32[4,512,256]{2,1,0:T(8,128)S(1)}, f32[4,512,256]{2,1,0:T(8,128)}, u32[]{:S(2)}) copy-start(f32[4,512,256]{2,1,0:T(8,128)} %get-tuple-element.166) | copy-start | bytes 6291460 | tf_op jit(solution)/shard_map/while
  76.8 2.2 %copy-start.1 = (f32[4,512,256]{2,1,0:T(8,128)S(1)}, f32[4,512,256]{2,1,0:T(8,128)}, u32[]{:S(2)}) copy-start(f32[4,512,256]{2,1,0:T(8,128)} %get-tuple-element.166) | copy-start | bytes 6291460 | tf_op jit(solution)/shard_map/while
  79.5 26.6 %copy-start.3 = (bf16[64,1024]{1,0:T(8,128)(2,1)S(1)}, bf16[64,1024]{1,0:T(8,128)(2,1)}, u32[]{:S(2)}) copy-start(bf16[64,1024]{1,0:T(8,128)(2,1)} %reduce-scatter.3.cloned.1.call-done) | copy-start | bytes 393220
  79.5 26.6 %copy-start.6 = (pred[64]{0:T(512)(128)(4,1)S(1)}, pred[64]{0:T(512)(128)(4,1)}, u32[]{:S(2)}) copy-start(pred[64]{0:T(512)(128)(4,1)} %copy-done.5) | copy-start | bytes 196
  79.6 28.0 %copy-start.8 = (f32[1024]{0:T(1024)S(1)}, f32[1024]{0:T(1024)}, u32[]{:S(2)}) copy-start(f32[1024]{0:T(1024)} %param.17) | copy-start | bytes 12292
  79.6 44.1 %copy-start.2 = (bf16[256,1024]{1,0:T(8,128)(2,1)S(1)}, bf16[256,1024]{1,0:T(8,128)(2,1)}, u32[]{:S(2)}) copy-start(bf16[256,1024]{1,0:T(8,128)(2,1)} %param.15) | copy-start | bytes 1572868
  81.0 61.9 %copy-start.10 = (pred[256]{0:T(512)(128)(4,1)S(1)}, pred[256]{0:T(512)(128)(4,1)}, u32[]{:S(2)}) copy-start(pred[256]{0:T(512)(128)(4,1)} %copy-done.9) | copy-start | bytes 772
Sparse Core Ops, SparseCore 0:
  10.5 24.5 reduce-scatter.2
  81.1 24.9 reduce-scatter.4
where the time goes:
time: 161 us
  blocking collectives  70.9 us (44%)
  waiting for transfers between devices  49 us (30%)
  between operations  16.3 us (10%)
  other arithmetic  12.8 us (8%)
  matrix products  9.33 us (6%)
  local copies, waits for them, and re-layouts  1.99 us (1%)
    reduce_scatter x1, waiting for transfers between devices, body(): lax.psum_scatter(jnp.dot(context, w_out, preferred_element_type=jnp.float...  25.1 us
    reduce_scatter x1, waiting for transfers between devices, body(): lax.psum_scatter(jnp.dot(onehot, table, preferred_element_type=jnp.float3...  23.9 us
    all_gather x1, blocking collectives, body(): lax.all_gather(final_local, 'mp', axis=0, tiled=True)  16 us
    all_gather x1, blocking collectives, body(): lax.all_gather(normed, 'mp', axis=0, tiled=True)  15.5 us
    psum x1, blocking collectives, body(): lax.psum(jnp.sum(jnp.exp(logits - row_max[:, None]), axis=-1), 'mp')  10.4 us
    pmax x1, blocking collectives, body(): row_max = lax.pmax(local_max, 'mp')  8.37 us
    all_gather x1, blocking collectives, body(): lax.all_gather(values, 'tm', axis=0, tiled=True)  7.28 us
    all_gather x1, blocking collectives, body(): lax.all_gather(keys, 'tm', axis=0, tiled=True)  7.14 us
  transfers between devices with their start and end apart: 2, of which 2 were waited for; matrix products, arithmetic and copies ran while one was open for 0% of the time, Pallas kernels for 0%

commit v1 on v0

v1 whole, which is shorter than its diff:
```python
import functools

import jax
import jax.numpy as jnp
from jax import lax
from jax.experimental import pallas as pl
from jax.experimental.pallas import tpu as pltpu
from jax.sharding import PartitionSpec as P

HEAD_DIM = 64
PLANE = ("clip", "tm")
NT = (((1,), (1,)), ((), ()))


def shape(dims, dtype):
    return jax.ShapeDtypeStruct(dims, dtype)


def layer_norm(values, gain):
    center = values - jnp.mean(values, axis=-1, keepdims=True)
    spread = jnp.mean(center * center, axis=-1, keepdims=True)
    return center * lax.rsqrt(spread + 1e-05) * gain


def flip(value, mask, count):
    return lax.ppermute(value, PLANE, [(i, i ^ mask) for i in range(count)])


def turn(value, shift, parts):
    return lax.ppermute(value, "mp", [(i, (i + shift) % parts) for i in range(parts)])


def front_kernel(ids_ref, masked_ref, vocab_ref, own_ref, near_ref, far_ref, place_ref, embed_ref,
                 gain_ref, w_ref, query_ref, pair_ref, mine_ref, held):
    ids = ids_ref[...]
    first = 0
    looked = None
    for part in (own_ref, near_ref, far_ref):
        rows = part.shape[0]
        onehot = jnp.where(ids == vocab_ref[:, first:first + rows], 1.0, 0.0).astype(jnp.bfloat16)
        term = jnp.dot(onehot, part[...], preferred_element_type=jnp.float32)
        looked = term if looked is None else looked + term
        first += rows
    hidden = jnp.where(masked_ref[...] > 0, embed_ref[...].astype(jnp.float32), looked)
    hidden = hidden + place_ref[...].astype(jnp.float32)
    held[...] = hidden
    normed = layer_norm(hidden, gain_ref[...]).astype(jnp.bfloat16)
    width = w_ref.shape[2]
    query = jnp.dot(normed, w_ref[0], preferred_element_type=jnp.float32)
    query_ref[...] = query.astype(jnp.bfloat16)
    for j in range(2):
        rows = jnp.dot(normed, w_ref[j + 1], preferred_element_type=jnp.float32)
        pair_ref[:, j * width:(j + 1) * width] = rows.astype(jnp.bfloat16)
    share = mine_ref.shape[0]
    start = pl.multiple_of(lax.axis_index("mp") * share, share)
    mine_ref[...] = held[pl.ds(start, share), :]


def attend_kernel(query_ref, *refs):
    parts = lax.axis_size("mp")
    blocks, w_ref, outs, total = refs[:-parts - 2], refs[-parts - 2], refs[-parts - 1:-1], refs[-1]
    rows, width = query_ref.shape
    lanes = 2 * HEAD_DIM
    column = lax.broadcasted_iota(jnp.int32, (rows, lanes), 1)
    context = []
    for first in range(0, width, lanes):
        query = query_ref[:, first:first + lanes] * jnp.bfloat16(HEAD_DIM ** -0.5)
        pair = []
        for head in range(2):
            here = (column < HEAD_DIM) if head == 0 else (column >= HEAD_DIM)
            asked = jnp.where(here, query, jnp.zeros_like(query))
            scores = [
                lax.dot_general(asked, ref[:, first:first + lanes], NT, preferred_element_type=jnp.float32)
                for ref in blocks
            ]
            highest = functools.reduce(jnp.maximum, [jnp.max(s, axis=-1, keepdims=True) for s in scores])
            weights = [jnp.exp(s - highest) for s in scores]
            summed = sum(jnp.sum(w, axis=-1, keepdims=True) for w in weights)
            mixed = sum(
                jnp.dot(w.astype(jnp.bfloat16), ref[:, width + first:width + first + lanes],
                        preferred_element_type=jnp.float32)
                for w, ref in zip(weights, blocks)
            )
            pair.append(mixed / summed)
        context.append(jnp.where(column < HEAD_DIM, pair[0], pair[1]).astype(jnp.bfloat16))
    total[...] = jnp.dot(jnp.concatenate(context, axis=1), w_ref[...], preferred_element_type=jnp.float32)
    me = lax.axis_index("mp")
    for shift, out in enumerate(outs):
        share = out.shape[0]
        start = pl.multiple_of(lax.rem(me + shift, parts) * share, share)
        out[...] = total[pl.ds(start, share), :].astype(out.dtype)


def final_kernel(mine_ref, hidden_ref, gain_ref, table_ref, *refs):
    parts = lax.axis_size("mp")
    others, outs, held = refs[:parts - 1], refs[parts - 1:-1], refs[-1]
    mixed = mine_ref[...]
    for other in others:
        mixed = mixed + other[...].astype(jnp.float32)
    rows = layer_norm(hidden_ref[...] + mixed, gain_ref[...]).astype(jnp.bfloat16)
    logits = lax.dot_general(rows, table_ref[...], NT, preferred_element_type=jnp.float32)
    highest = jnp.max(logits, axis=-1, keepdims=True)
    log_total = highest + jnp.log(jnp.sum(jnp.exp(logits - highest), axis=-1, keepdims=True))
    held[...] = (logits - log_total).astype(jnp.bfloat16)
    confidence = jnp.exp(highest - log_total)
    share = logits.shape[0]
    width = outs[0].shape[1]
    me = lax.axis_index("mp")
    row = lax.broadcasted_iota(jnp.int32, (share, width), 0) + me * share
    lane = lax.broadcasted_iota(jnp.int32, (share, width), 1)
    line = jnp.sum(jnp.where(row == lane, confidence, 0.0), axis=0, keepdims=True)
    high = line.astype(jnp.bfloat16)
    rest = line - high.astype(jnp.float32)
    middle = rest.astype(jnp.bfloat16)
    low = (rest - middle.astype(jnp.float32)).astype(jnp.bfloat16)
    extra = outs[0].shape[0] - share
    place = lax.broadcasted_iota(jnp.int32, (extra, width), 0)
    tail = jnp.where(place == 0, high.astype(jnp.float32),
                     jnp.where(place == 1, middle.astype(jnp.float32),
                               jnp.where(place == 2, low.astype(jnp.float32), 0.0))).astype(jnp.bfloat16)
    for shift, out in enumerate(outs):
        start = pl.multiple_of(lax.rem(me + shift, parts) * width, width)
        out[:share, :] = held[:, pl.ds(start, width)]
        out[share:, :] = tail


def close_kernel(masked_ref, *refs):
    parts = lax.axis_size("mp")
    pieces, log_ref, conf_ref, sums_ref = refs[:parts], refs[-3], refs[-2], refs[-1]
    me = lax.axis_index("mp")
    share = log_ref.shape[0] // parts
    line = None
    for shift, piece in enumerate(pieces):
        start = pl.multiple_of(lax.rem(me + parts - shift, parts) * share, share)
        log_ref[pl.ds(start, share), :] = piece[:share, :]
        tail = piece[share:, :].astype(jnp.float32)
        term = jnp.sum(tail, axis=0, keepdims=True)
        line = term if line is None else line + term
    conf_ref[...] = line
    weight = masked_ref[...]
    lanes = sums_ref.shape[1]
    side = lax.broadcasted_iota(jnp.int32, (1, lanes), 1)
    sums_ref[...] = jnp.where(
        side == 0, jnp.sum(line * weight), jnp.where(side == 1, jnp.sum(weight), 0.0)
    )


def body(token_ids, remask, position_embed, mask_embed, table, gain_in, gain_out, w_qkv, w_out):
    bf16, f32 = jnp.bfloat16, jnp.float32
    frames_here, span = token_ids.shape
    rows = frames_here * span
    parts = lax.axis_size("mp")
    clips, tms = lax.axis_size("clip"), lax.axis_size("tm")
    plane = clips * tms
    clip, tm, me = lax.axis_index("clip"), lax.axis_index("tm"), lax.axis_index("mp")
    vocab_here, depth = table.shape
    width = w_qkv.shape[2]
    share = rows // parts

    masks = [m for m in (1, 2) if tms % (2 * m) == 0] + ([tms] if clips % 2 == 0 else [])
    spot = clip * tms + tm
    piece = sum(jnp.where((spot & m) > 0, 1 << b, 0) for b, m in enumerate(masks))
    cuts = 1 << len(masks)
    cut = vocab_here // cuts

    sent = lax.dynamic_slice_in_dim(table, piece * cut, cut, 0)
    got = jnp.concatenate([turn(sent, s, parts) for s in range(1, parts)], axis=0)
    combos = [c for c in range(0, cuts, 2)]
    near = [got]
    for c in combos[1:]:
        mask = sum(m for b, m in enumerate(masks) if c >> b & 1)
        near.append(flip(got, mask, plane))
    near = jnp.concatenate(near, axis=0)
    far = flip(near, masks[0], plane)

    sources = jnp.stack([(me + parts - s) % parts for s in range(1, parts)])
    inner = jnp.arange(cut, dtype=jnp.int32)

    def listing(odd):
        rows_of = [piece ^ (c + odd) for c in combos]
        return jnp.concatenate([
            (sources[:, None] * vocab_here + p * cut + inner[None, :]).reshape(-1) for p in rows_of
        ])

    vocab = jnp.concatenate(
        [me * vocab_here + jnp.arange(vocab_here, dtype=jnp.int32), listing(0), listing(1)]
    ).astype(jnp.int32)[None, :]

    spots = jnp.arange(span, dtype=jnp.int32)
    masked = jnp.any(remask[:, None, :] == spots[None, :, None], axis=-1).reshape(rows)
    weight = masked.astype(f32)
    ids = jnp.where(masked, -1, token_ids.reshape(rows))

    query, pair, mine = pl.pallas_call(
        front_kernel,
        out_shape=[shape((rows, width), bf16), shape((rows, 2 * width), bf16), shape((share, depth), f32)],
        scratch_shapes=[pltpu.VMEM((rows, depth), f32)],
    )(ids[:, None], masked.astype(jnp.int32)[:, None], vocab, table, near, far,
      position_embed.reshape(rows, depth), mask_embed[None, :], gain_in[None, :], w_qkv)

    blocks = [pair]
    mask = tms // 2
    held = pair
    while mask >= 1:
        other = flip(held, mask, plane)
        blocks.append(other)
        held = jnp.concatenate([held, other], axis=0)
        mask //= 2

    whole = jnp.zeros((parts * vocab_here, depth), bf16)
    whole = lax.dynamic_update_slice(whole, table, (me * vocab_here, 0))
    for odd, part in ((0, near), (1, far)):
        chunks = part.reshape(len(combos), parts - 1, cut, depth)
        for i, c in enumerate(combos):
            for s in range(1, parts):
                at = ((me + parts - s) % parts) * vocab_here + (piece ^ (c + odd)) * cut
                whole = lax.dynamic_update_slice(whole, chunks[i, s - 1], (at, 0))

    sums = pl.pallas_call(
        attend_kernel,
        out_shape=[shape((share, depth), f32)] + [shape((share, depth), bf16)] * (parts - 1),
        scratch_shapes=[pltpu.VMEM((rows, depth), f32)],
    )(query, *blocks, w_out)
    others = [turn(sums[s], s, parts) for s in range(1, parts)]

    extra = 16
    notes = pl.pallas_call(
        final_kernel,
        out_shape=[shape((share + extra, vocab_here), bf16)] * parts,
        scratch_shapes=[pltpu.VMEM((share, parts * vocab_here), bf16)],
    )(sums[0], mine, gain_out[None, :], whole, *others)
    notes = [notes[0]] + [turn(notes[s], s, parts) for s in range(1, parts)]
    log_probs, confidence, stats = pl.pallas_call(
        close_kernel,
        out_shape=[shape((rows, vocab_here), bf16), shape((1, rows), f32), shape((1, 128), f32)],
    )(weight[None, :], *notes)
    mask = 1
    while mask < tms:
        stats = stats + flip(stats, mask, plane)
        mask *= 2
    conf_sum, count = stats[0, 0], stats[0, 1]
    clip_stats = jnp.stack([conf_sum / count, jnp.log(count / (rows * tms))])
    return (
        log_probs.reshape(frames_here, span, vocab_here),
        confidence.reshape(frames_here, span),
        clip_stats,
    )


def solution(mesh):
    return jax.shard_map(
        body,
        mesh=mesh,
        in_specs=(
            P(("clip", "tm"), None),
            P(("clip", "tm"), None),
            P("tm", None, None),
            P(),
            P("mp", None),
            P(),
            P(),
            P(None, None, "mp"),
            P("mp", None),
        ),
        out_specs=(P(("clip", "tm"), None, "mp"), P(("clip", "tm"), None), P("clip")),
        check_vma=False,
    )
```

time: 161 us -> 91.5 us (0.57)
  blocking collectives: 70.9 us -> 0 us
  waiting for transfers between devices: 49 us -> 25.7 us
  starting transfers between devices: 0.08 us -> 20.4 us
  local copies, waits for them, and re-layouts: 1.99 us -> 22.1 us
  Pallas kernels: 0 us -> 14.6 us
  between operations: 16.3 us -> 2.88 us
  matrix products: 9.33 us -> 0 us
  other arithmetic: 12.8 us -> 4.91 us
    reduce_scatter x2 -> x0, waiting for transfers between devices: 49 us -> none  [the longest x1 25.1 us: body(): lax.psum_scatter(jnp.dot(context, w_out, preferred_element_type=jnp.float...]
    all_gather x4 -> x0, blocking collectives: 45.9 us -> none  [the longest x1 16 us: body(): lax.all_gather(final_local, 'mp', axis=0, tiled=True)]
    ppermute x0 -> x17, waiting for transfers between devices: none -> 25.7 us  [the longest x8 14.4 us: flip(): return lax.ppermute(value, PLANE, [(i, i ^ mask) for i in range(count)])]
    ppermute x0 -> x17, starting transfers between devices: none -> 20.4 us  [the longest x9 15.6 us: turn(): lax.ppermute(value, 'mp', [(i, (i + shift) % parts) for i in range(parts)])]
    psum x2 -> x0, blocking collectives: 16.6 us -> none  [the longest x1 10.4 us: body(): lax.psum(jnp.sum(jnp.exp(logits - row_max[:, None]), axis=-1), 'mp')]
    pallas_call x0 -> x4, Pallas kernels: none -> 14.6 us  [the longest x1 4.92 us: body(): pl.pallas_call(front_kernel, out_shape=[shape((rows, width), bf16), shape...]
    dynamic_update_slice x0 -> x25, local copies, waits for them, and re-layouts: none -> 10.3 us  [the longest x24 10.3 us: body(): whole = lax.dynamic_update_slice(whole, chunks[i, s - 1], (at, 0))]
    dot_general x8 -> x0, matrix products: 9.33 us -> none  [the longest x2 3.69 us: absorb_block(): jnp.einsum('qhd,khd->hqk', query, key_block, preferred_element_type=jnp.f...]
  transfers between devices with their start and end apart: 2 -> 17, of which waited for: 2 -> 9; matrix products, arithmetic and copies ran while one was open for 0% -> 22% of each run, Pallas kernels for 0% -> 0%
where the time goes in v1:
time: 91.5 us; the launch traced here: 90.6 us
  waiting for transfers between devices  25.7 us (28%)
  local copies, waits for them, and re-layouts  22.1 us (24%)
  starting transfers between devices  20.4 us (22%)
  Pallas kernels  14.6 us (16%)
  other arithmetic  4.91 us (5%)
  between operations  2.88 us (3%)
    ppermute x9, starting transfers between devices, turn(): lax.ppermute(value, 'mp', [(i, (i + shift) % parts) for i in range(parts)])  15.6 us
    ppermute x8, waiting for transfers between devices, flip(): return lax.ppermute(value, PLANE, [(i, i ^ mask) for i in range(count)])  14.4 us
    ppermute x9, waiting for transfers between devices, turn(): lax.ppermute(value, 'mp', [(i, (i + shift) % parts) for i in range(parts)])  11.3 us
    dynamic_update_slice x24, local copies, waits for them, and re-layouts, body(): whole = lax.dynamic_update_slice(whole, chunks[i, s - 1], (at, 0))  10.3 us
    unnamed x28, local copies, waits for them, and re-layouts  5.17 us
    pallas_call x1, Pallas kernels, body(): pl.pallas_call(front_kernel, out_shape=[shape((rows, width), bf16), shape...  4.92 us
    ppermute x8, starting transfers between devices, flip(): return lax.ppermute(value, PLANE, [(i, i ^ mask) for i in range(count)])  4.78 us
    pallas_call x1, Pallas kernels, body(): pl.pallas_call(attend_kernel, out_shape=[shape((share, depth), f32)] + [s...  4.56 us
  transfers between devices with their start and end apart: 17, of which 9 were waited for; matrix products, arithmetic and copies ran while one was open for 22% of the time, Pallas kernels for 0%

profile of v1, /device:TPU:0, one launch (start us, length us, event | category | flops | bytes accessed | tf_op | source)
XLA Modules:
  0.0 90.6 jit_solution(12664123785113039554)
XLA Ops:
  1.6 3.1 %collective-permute-start = (bf16[32,1024]{1,0:T(8,128)(2,1)S(1)}, bf16[32,1024]{1,0:T(8,128)(2,1)S(1)}, u32[]{:S(2)}, u32[]{:S(2)}) collective-permute-start(bf16[32,1024]{1,0:T(8,128)(2,1)S(1)} %constant_dynamic-slice_fusion), channel_id=1, source_target_pairs={{0,1},{1,2},{2,3},{3,0},{4,5},{5,6},{6,7},{7,4},{8,9},{9,10},{10,1... | collective-permute-start | bytes 196616 | tf_op jit(solution)/shard_map/ppermute | solution.py:30
  4.6 2.6 %collective-permute-start.1 = (bf16[32,1024]{1,0:T(8,128)(2,1)S(1)}, bf16[32,1024]{1,0:T(8,128)(2,1)S(1)}, u32[]{:S(2)}, u32[]{:S(2)}) collective-permute-start(bf16[32,1024]{1,0:T(8,128)(2,1)S(1)} %constant_dynamic-slice_fusion), channel_id=1, source_target_pairs={{0,2},{1,3},{2,0},{3,1},{4,6},{5,7},{6,4},{7,5},{8,10},{9,11},{10,... | collective-permute-start | bytes 196616 | tf_op jit(solution)/shard_map/ppermute | solution.py:30
  7.2 1.3 %collective-permute-start.2 = (bf16[32,1024]{1,0:T(8,128)(2,1)S(1)}, bf16[32,1024]{1,0:T(8,128)(2,1)S(1)}, u32[]{:S(2)}, u32[]{:S(2)}) collective-permute-start(bf16[32,1024]{1,0:T(8,128)(2,1)S(1)} %constant_dynamic-slice_fusion), channel_id=1, source_target_pairs={{0,3},{1,0},{2,1},{3,2},{4,7},{5,4},{6,5},{7,6},{8,11},{9,8},{10,9... | collective-permute-start | bytes 196616 | tf_op jit(solution)/shard_map/ppermute | solution.py:30
  12.9 1.3 %broadcast_in_dim.15.embed_ref = bf16[1,1024]{1,0:T(2,128)(2,1)} reshape(bf16[1024]{0:T(1024)(128)(2,1)} %param.12) | data formatting | bytes 4096 | tf_op jit(solution)/shard_map/broadcast_in_dim | solution.py:199
  16.0 1.5 %collective-permute-start.3 = (bf16[96,1024]{1,0:T(8,128)(2,1)}, bf16[96,1024]{1,0:T(8,128)(2,1)}, u32[]{:S(2)}, u32[]{:S(2)}) collective-permute-start(bf16[96,1024]{1,0:T(8,128)(2,1)} %get-tuple-element.33), channel_id=1, source_target_pairs={{0,8},{4,12},{8,0},{12,4},{16,24},{20,28},{24,16},{28,20},{1,9},{5... | collective-permute-start | bytes 589832 | tf_op jit(solution)/shard_map/ppermute | solution.py:26
  18.2 1.5 %collective-permute-start.4 = (bf16[96,1024]{1,0:T(8,128)(2,1)}, bf16[96,1024]{1,0:T(8,128)(2,1)S(1)}, u32[]{:S(2)}, u32[]{:S(2)}) collective-permute-start(bf16[96,1024]{1,0:T(8,128)(2,1)} %get-tuple-element.33), channel_id=1, source_target_pairs={{0,16},{4,20},{8,24},{12,28},{16,0},{20,4},{24,8},{28,12},{1,17},{... | collective-permute-start | bytes 589832 | tf_op jit(solution)/shard_map/ppermute | solution.py:26
  20.6 2.3 %collective-permute-done.3 = bf16[96,1024]{1,0:T(8,128)(2,1)} collective-permute-done((bf16[96,1024]{1,0:T(8,128)(2,1)}, bf16[96,1024]{1,0:T(8,128)(2,1)}, u32[]{:S(2)}, u32[]{:S(2)}) %collective-permute-start.3) | collective-permute-done | bytes 196640 | tf_op jit(solution)/shard_map/ppermute | solution.py:26
  22.9 0.9 %constant_dynamic-update-slice_fusion.5 = bf16[384,1024]{1,0:T(8,128)(2,1)S(1)} fusion(bf16[384,1024]{1,0:T(8,128)(2,1)S(1)} %get-tuple-element.34, bf16[96,1024]{1,0:T(8,128)(2,1)} %collective-permute-done.3), kind=kLoop, calls=%fused_computation.57 | loop fusion | bytes 393216
  23.8 4.4 %collective-permute-done.4 = bf16[96,1024]{1,0:T(8,128)(2,1)S(1)} collective-permute-done((bf16[96,1024]{1,0:T(8,128)(2,1)}, bf16[96,1024]{1,0:T(8,128)(2,1)S(1)}, u32[]{:S(2)}, u32[]{:S(2)}) %collective-permute-start.4) | collective-permute-done | bytes 196640 | tf_op jit(solution)/shard_map/ppermute | solution.py:26
  28.7 2.0 %collective-permute-done.6.far_ref = bf16[384,1024]{1,0:T(8,128)(2,1)S(1)} collective-permute-done((bf16[384,1024]{1,0:T(8,128)(2,1)S(1)}, bf16[384,1024]{1,0:T(8,128)(2,1)S(1)}, u32[]{:S(2)}, u32[]{:S(2)}) %collective-permute-start.6) | collective-permute-done | bytes 786464 | tf_op jit(solution)/shard_map/ppermute | solution.py:26
  31.6 4.9 %shard_map.112 = (bf16[256,256]{1,0:T(8,128)(2,1)}, bf16[256,512]{1,0:T(8,128)(2,1)}, f32[64,1024]{1,0:T(8,128)}) custom-call(s32[256,1]{1,0:T(8,128)} %broadcast_select_fusion.ids_ref, s32[256,1]{1,0:T(8,128)} %copy.20.masked_ref, s32[1,1024]{1,0:T(1,128)} %bitcast.136, bf16[256,1024]{1,0:T(8,128)(2,1)} %own_ref.1, bf16[384,1024]{1,0:T(8,128)(2,1)} %copy-done.1, ...), custom_call_target="tpu_custom_call" | custom-call | tf_op jit(solution)/shard_map/pallas_call | solution.py:194
  43.8 1.3 %collective-permute-done.7.refs_1_ = bf16[256,512]{1,0:T(8,128)(2,1)S(1)} collective-permute-done((bf16[256,512]{1,0:T(8,128)(2,1)}, bf16[256,512]{1,0:T(8,128)(2,1)S(1)}, u32[]{:S(2)}, u32[]{:S(2)}) %collective-permute-start.7) | collective-permute-done | bytes 262176 | tf_op jit(solution)/shard_map/ppermute | solution.py:26
  45.1 1.1 %pad_maximum_fusion = bf16[512,512]{1,0:T(8,128)(2,1)S(1)} fusion(bf16[256,512]{1,0:T(8,128)(2,1)S(1)} %collective-permute-done.7.refs_1_, bf16[256,512]{1,0:T(8,128)(2,1)} %get-tuple-element.18.refs_0_), kind=kLoop, calls=%fused_computation | loop fusion | flops 1048576 | bytes 1048576 | tf_op jit(solution)/shard_map/concatenate | solution.py:207
  49.6 4.6 %shard_map.113 = (f32[64,1024]{1,0:T(8,128)}, bf16[64,1024]{1,0:T(8,128)(2,1)}, bf16[64,1024]{1,0:T(8,128)(2,1)}, bf16[64,1024]{1,0:T(8,128)(2,1)}) custom-call(bf16[256,256]{1,0:T(8,128)(2,1)} %get-tuple-element.17.query_ref, bf16[256,512]{1,0:T(8,128)(2,1)} %get-tuple-element.18.refs_0_, bf16[256,512]{1,0:T(8,128)(2,1)} %copy-done.4, ...), custom_call_target="tpu_custom_call" | custom-call | tf_op jit(solution)/shard_map/pallas_call | solution.py:219
  54.5 2.7 %collective-permute-start.11 = (bf16[64,1024]{1,0:T(8,128)(2,1)}, bf16[64,1024]{1,0:T(8,128)(2,1)S(1)}, u32[]{:S(2)}, u32[]{:S(2)}) collective-permute-start(bf16[64,1024]{1,0:T(8,128)(2,1)} %get-tuple-element.23), channel_id=1, source_target_pairs={{0,3},{1,0},{2,1},{3,2},{4,7},{5,4},{6,5},{7,6},{8,11},{9,8},{10,9... | collective-permute-start | bytes 393224 | tf_op jit(solution)/shard_map/ppermute | solution.py:30
  58.0 6.6 %collective-permute-done.10.refs_1_ = bf16[64,1024]{1,0:T(8,128)(2,1)S(1)} collective-permute-done((bf16[64,1024]{1,0:T(8,128)(2,1)}, bf16[64,1024]{1,0:T(8,128)(2,1)S(1)}, u32[]{:S(2)}, u32[]{:S(2)}) %collective-permute-start.10) | collective-permute-done | bytes 131104 | tf_op jit(solution)/shard_map/ppermute | solution.py:30
  64.6 2.4 %collective-permute-done.9.refs_0_ = bf16[64,1024]{1,0:T(8,128)(2,1)S(1)} collective-permute-done((bf16[64,1024]{1,0:T(8,128)(2,1)}, bf16[64,1024]{1,0:T(8,128)(2,1)S(1)}, u32[]{:S(2)}, u32[]{:S(2)}) %collective-permute-start.9) | collective-permute-done | bytes 131104 | tf_op jit(solution)/shard_map/ppermute | solution.py:30
  67.7 3.6 %shard_map.114 = (bf16[80,256]{1,0:T(8,128)(2,1)}, bf16[80,256]{1,0:T(8,128)(2,1)}, bf16[80,256]{1,0:T(8,128)(2,1)}, bf16[80,256]{1,0:T(8,128)(2,1)}) custom-call(f32[64,1024]{1,0:T(8,128)} %get-tuple-element.19.mine_ref, f32[64,1024]{1,0:T(8,128)} %get-tuple-element.20.hidden_ref, f32[1,1024]{1,0:T(1,128)} %bitcast.138, bf16[1024,1024]{1,0:T(8,128)(2,1)} %copy-done, ...), custom_call_target="tpu_custom_call" | custom-call | tf_op jit(solution)/shard_map/pallas_call | solution.py:227
  71.3 3.2 %collective-permute-start.12 = (bf16[80,256]{1,0:T(8,128)(2,1)}, bf16[80,256]{1,0:T(8,128)(2,1)S(1)}, u32[]{:S(2)}, u32[]{:S(2)}) collective-permute-start(bf16[80,256]{1,0:T(8,128)(2,1)} %get-tuple-element.25), channel_id=1, source_target_pairs={{0,1},{1,2},{2,3},{3,0},{4,5},{5,6},{6,7},{7,4},{8,9},{9,10},{10,1... | collective-permute-start | bytes 122888 | tf_op jit(solution)/shard_map/ppermute | solution.py:30
  74.4 2.4 %collective-permute-start.14 = (bf16[80,256]{1,0:T(8,128)(2,1)}, bf16[80,256]{1,0:T(8,128)(2,1)S(1)}, u32[]{:S(2)}, u32[]{:S(2)}) collective-permute-start(bf16[80,256]{1,0:T(8,128)(2,1)} %get-tuple-element.27), channel_id=1, source_target_pairs={{0,3},{1,0},{2,1},{3,2},{4,7},{5,4},{6,5},{7,6},{8,11},{9,8},{10,9... | collective-permute-start | bytes 122888 | tf_op jit(solution)/shard_map/ppermute | solution.py:30
  77.4 2.3 %collective-permute-done.13.refs_2_ = bf16[80,256]{1,0:T(8,128)(2,1)S(1)} collective-permute-done((bf16[80,256]{1,0:T(8,128)(2,1)}, bf16[80,256]{1,0:T(8,128)(2,1)S(1)}, u32[]{:S(2)}, u32[]{:S(2)}) %collective-permute-start.13) | collective-permute-done | bytes 40992 | tf_op jit(solution)/shard_map/ppermute | solution.py:30
  80.3 1.5 %shard_map.115 = (bf16[256,256]{1,0:T(8,128)(2,1)}, f32[1,256]{1,0:T(1,128)}, f32[1,128]{1,0:T(1,128)}) custom-call(f32[1,256]{1,0:T(1,128)} %bitcast.140, bf16[80,256]{1,0:T(8,128)(2,1)} %get-tuple-element.24.refs_0_, bf16[80,256]{1,0:T(8,128)(2,1)} %copy-done.9, bf16[80,256]{1,0:T(8,128)(2,1)} %copy-done.10, bf16[80,256]{1,0:T(8,128)(2,1)} %copy-done.11), custom_call_target="tpu_custom_call" | custom-call | tf_op jit(solution)/shard_map/pallas_call | solution.py:233
  81.8 1.3 %collective-permute-done.15 = f32[1,128]{1,0:T(1,128)S(1)} collective-permute-done((f32[1,128]{1,0:T(1,128)}, f32[1,128]{1,0:T(1,128)S(1)}, u32[]{:S(2)}, u32[]{:S(2)}) %collective-permute-start.15) | collective-permute-done | bytes 544 | tf_op jit(solution)/shard_map/ppermute | solution.py:26
  84.3 3.0 %collective-permute-done.16 = f32[1,128]{1,0:T(1,128)S(1)} collective-permute-done((f32[1,128]{1,0:T(1,128)S(1)}, f32[1,128]{1,0:T(1,128)S(1)}, u32[]{:S(2)}, u32[]{:S(2)}) %collective-permute-start.16) | collective-permute-done | bytes 544 | tf_op jit(solution)/shard_map/ppermute | solution.py:26
  (100 shorter events, 25.9 us)
Async XLA Ops:
  0.6 19.3 %copy-start.3 = (bf16[256,1024]{1,0:T(8,128)(2,1)S(1)}, bf16[256,1024]{1,0:T(8,128)(2,1)}, u32[]{:S(2)}) copy-start(bf16[256,1024]{1,0:T(8,128)(2,1)} %own_ref.1) | copy-start | bytes 1572868
  1.6 12.6 %collective-permute-start = (bf16[32,1024]{1,0:T(8,128)(2,1)S(1)}, bf16[32,1024]{1,0:T(8,128)(2,1)S(1)}, u32[]{:S(2)}, u32[]{:S(2)}) collective-permute-start(bf16[32,1024]{1,0:T(8,128)(2,1)S(1)} %constant_dynamic-slice_fusion), channel_id=1, source_target_pairs={{0,1},{1,2},{2,3},{3,0},{4,5},{5,6},{6,7},{7,4},{8,9},{9,10},{10,1... | collective-permute-start | bytes 196616 | tf_op jit(solution)/shard_map/ppermute | solution.py:30
  4.6 10.2 %collective-permute-start.1 = (bf16[32,1024]{1,0:T(8,128)(2,1)S(1)}, bf16[32,1024]{1,0:T(8,128)(2,1)S(1)}, u32[]{:S(2)}, u32[]{:S(2)}) collective-permute-start(bf16[32,1024]{1,0:T(8,128)(2,1)S(1)} %constant_dynamic-slice_fusion), channel_id=1, source_target_pairs={{0,2},{1,3},{2,0},{3,1},{4,6},{5,7},{6,4},{7,5},{8,10},{9,11},{10,... | collective-permute-start | bytes 196616 | tf_op jit(solution)/shard_map/ppermute | solution.py:30
  7.2 8.2 %collective-permute-start.2 = (bf16[32,1024]{1,0:T(8,128)(2,1)S(1)}, bf16[32,1024]{1,0:T(8,128)(2,1)S(1)}, u32[]{:S(2)}, u32[]{:S(2)}) collective-permute-start(bf16[32,1024]{1,0:T(8,128)(2,1)S(1)} %constant_dynamic-slice_fusion), channel_id=1, source_target_pairs={{0,3},{1,0},{2,1},{3,2},{4,7},{5,4},{6,5},{7,6},{8,11},{9,8},{10,9... | collective-permute-start | bytes 196616 | tf_op jit(solution)/shard_map/ppermute | solution.py:30
  16.0 6.9 %collective-permute-start.3 = (bf16[96,1024]{1,0:T(8,128)(2,1)}, bf16[96,1024]{1,0:T(8,128)(2,1)}, u32[]{:S(2)}, u32[]{:S(2)}) collective-permute-start(bf16[96,1024]{1,0:T(8,128)(2,1)} %get-tuple-element.33), channel_id=1, source_target_pairs={{0,8},{4,12},{8,0},{12,4},{16,24},{20,28},{24,16},{28,20},{1,9},{5... | collective-permute-start | bytes 589832 | tf_op jit(solution)/shard_map/ppermute | solution.py:26
  18.2 10.1 %collective-permute-start.4 = (bf16[96,1024]{1,0:T(8,128)(2,1)}, bf16[96,1024]{1,0:T(8,128)(2,1)S(1)}, u32[]{:S(2)}, u32[]{:S(2)}) collective-permute-start(bf16[96,1024]{1,0:T(8,128)(2,1)} %get-tuple-element.33), channel_id=1, source_target_pairs={{0,16},{4,20},{8,24},{12,28},{16,0},{20,4},{24,8},{28,12},{1,17},{... | collective-permute-start | bytes 589832 | tf_op jit(solution)/shard_map/ppermute | solution.py:26
  20.0 8.3 %collective-permute-start.5 = (bf16[96,1024]{1,0:T(8,128)(2,1)}, bf16[96,1024]{1,0:T(8,128)(2,1)S(1)}, u32[]{:S(2)}, u32[]{:S(2)}) collective-permute-start(bf16[96,1024]{1,0:T(8,128)(2,1)} %get-tuple-element.33), channel_id=1, source_target_pairs={{0,24},{4,28},{8,16},{12,20},{16,8},{20,12},{24,0},{28,4},{1,25},{... | collective-permute-start | bytes 589832 | tf_op jit(solution)/shard_map/ppermute | solution.py:26
  28.3 3.2 %copy-start.1 = (bf16[384,1024]{1,0:T(8,128)(2,1)}, bf16[384,1024]{1,0:T(8,128)(2,1)S(1)}, u32[]{:S(2)}) copy-start(bf16[384,1024]{1,0:T(8,128)(2,1)S(1)} %constant_dynamic-update-slice_fusion.3.near_ref) | copy-start | bytes 2359300
  28.3 2.4 %collective-permute-start.6 = (bf16[384,1024]{1,0:T(8,128)(2,1)S(1)}, bf16[384,1024]{1,0:T(8,128)(2,1)S(1)}, u32[]{:S(2)}, u32[]{:S(2)}) collective-permute-start(bf16[384,1024]{1,0:T(8,128)(2,1)S(1)} %constant_dynamic-update-slice_fusion.3.near_ref), channel_id=1, source_target_pairs={{0,4},{4,0},{8,12},{12,8},{16,20},{20,16},{24,28},{28,24},{1,5},{5... | collective-permute-start | bytes 2359304 | tf_op jit(solution)/shard_map/ppermute | solution.py:26
  36.5 8.6 %collective-permute-start.7 = (bf16[256,512]{1,0:T(8,128)(2,1)}, bf16[256,512]{1,0:T(8,128)(2,1)S(1)}, u32[]{:S(2)}, u32[]{:S(2)}) collective-permute-start(bf16[256,512]{1,0:T(8,128)(2,1)} %get-tuple-element.18.refs_0_), channel_id=1, source_target_pairs={{0,8},{4,12},{8,0},{12,4},{16,24},{20,28},{24,16},{28,20},{1,9},{5... | collective-permute-start | bytes 786440 | tf_op jit(solution)/shard_map/ppermute | solution.py:26
  45.1 3.7 %copy-start.4 = (bf16[256,512]{1,0:T(8,128)(2,1)}, bf16[256,512]{1,0:T(8,128)(2,1)S(1)}, u32[]{:S(2)}) copy-start(bf16[256,512]{1,0:T(8,128)(2,1)S(1)} %collective-permute-done.7.refs_1_) | copy-start | bytes 786436
  46.1 2.6 %collective-permute-start.8 = (bf16[512,512]{1,0:T(8,128)(2,1)S(1)}, bf16[512,512]{1,0:T(8,128)(2,1)S(1)}, u32[]{:S(2)}, u32[]{:S(2)}) collective-permute-start(bf16[512,512]{1,0:T(8,128)(2,1)S(1)} %pad_maximum_fusion), channel_id=1, source_target_pairs={{0,4},{4,0},{8,12},{12,8},{16,20},{20,16},{24,28},{28,24},{1,5},{5... | collective-permute-start | bytes 1572872 | tf_op jit(solution)/shard_map/ppermute | solution.py:26
  54.1 10.5 %collective-permute-start.10 = (bf16[64,1024]{1,0:T(8,128)(2,1)}, bf16[64,1024]{1,0:T(8,128)(2,1)S(1)}, u32[]{:S(2)}, u32[]{:S(2)}) collective-permute-start(bf16[64,1024]{1,0:T(8,128)(2,1)} %get-tuple-element.22), channel_id=1, source_target_pairs={{0,2},{1,3},{2,0},{3,1},{4,6},{5,7},{6,4},{7,5},{8,10},{9,11},{10,... | collective-permute-start | bytes 393224 | tf_op jit(solution)/shard_map/ppermute | solution.py:30
  54.5 10.2 %collective-permute-start.11 = (bf16[64,1024]{1,0:T(8,128)(2,1)}, bf16[64,1024]{1,0:T(8,128)(2,1)S(1)}, u32[]{:S(2)}, u32[]{:S(2)}) collective-permute-start(bf16[64,1024]{1,0:T(8,128)(2,1)} %get-tuple-element.23), channel_id=1, source_target_pairs={{0,3},{1,0},{2,1},{3,2},{4,7},{5,4},{6,5},{7,6},{8,11},{9,8},{10,9... | collective-permute-start | bytes 393224 | tf_op jit(solution)/shard_map/ppermute | solution.py:30
  57.2 9.8 %collective-permute-start.9 = (bf16[64,1024]{1,0:T(8,128)(2,1)}, bf16[64,1024]{1,0:T(8,128)(2,1)S(1)}, u32[]{:S(2)}, u32[]{:S(2)}) collective-permute-start(bf16[64,1024]{1,0:T(8,128)(2,1)} %get-tuple-element.21), channel_id=1, source_target_pairs={{0,1},{1,2},{2,3},{3,0},{4,5},{5,6},{6,7},{7,4},{8,9},{9,10},{10,1... | collective-permute-start | bytes 393224 | tf_op jit(solution)/shard_map/ppermute | solution.py:30
  58.0 9.0 %copy-start = (bf16[1024,1024]{1,0:T(8,128)(2,1)}, bf16[1024,1024]{1,0:T(8,128)(2,1)S(1)}, u32[]{:S(2)}) copy-start(bf16[1024,1024]{1,0:T(8,128)(2,1)S(1)} %fusion.1.table_ref) | copy-start | bytes 6291460
  64.6 2.4 %copy-start.6 = (bf16[64,1024]{1,0:T(8,128)(2,1)}, bf16[64,1024]{1,0:T(8,128)(2,1)S(1)}, u32[]{:S(2)}) copy-start(bf16[64,1024]{1,0:T(8,128)(2,1)S(1)} %collective-permute-done.10.refs_1_) | copy-start | bytes 393220
  64.6 2.4 %copy-start.7 = (bf16[64,1024]{1,0:T(8,128)(2,1)}, bf16[64,1024]{1,0:T(8,128)(2,1)S(1)}, u32[]{:S(2)}) copy-start(bf16[64,1024]{1,0:T(8,128)(2,1)S(1)} %collective-permute-done.11.refs_2_) | copy-start | bytes 393220
  71.3 6.1 %collective-permute-start.12 = (bf16[80,256]{1,0:T(8,128)(2,1)}, bf16[80,256]{1,0:T(8,128)(2,1)S(1)}, u32[]{:S(2)}, u32[]{:S(2)}) collective-permute-start(bf16[80,256]{1,0:T(8,128)(2,1)} %get-tuple-element.25), channel_id=1, source_target_pairs={{0,1},{1,2},{2,3},{3,0},{4,5},{5,6},{6,7},{7,4},{8,9},{9,10},{10,1... | collective-permute-start | bytes 122888 | tf_op jit(solution)/shard_map/ppermute | solution.py:30
  74.4 5.3 %collective-permute-start.13 = (bf16[80,256]{1,0:T(8,128)(2,1)}, bf16[80,256]{1,0:T(8,128)(2,1)S(1)}, u32[]{:S(2)}, u32[]{:S(2)}) collective-permute-start(bf16[80,256]{1,0:T(8,128)(2,1)} %get-tuple-element.26), channel_id=1, source_target_pairs={{0,2},{1,3},{2,0},{3,1},{4,6},{5,7},{6,4},{7,5},{8,10},{9,11},{10,... | collective-permute-start | bytes 122888 | tf_op jit(solution)/shard_map/ppermute | solution.py:30
  74.4 5.3 %collective-permute-start.14 = (bf16[80,256]{1,0:T(8,128)(2,1)}, bf16[80,256]{1,0:T(8,128)(2,1)S(1)}, u32[]{:S(2)}, u32[]{:S(2)}) collective-permute-start(bf16[80,256]{1,0:T(8,128)(2,1)} %get-tuple-element.27), channel_id=1, source_target_pairs={{0,3},{1,0},{2,1},{3,2},{4,7},{5,4},{6,5},{7,6},{8,11},{9,8},{10,9... | collective-permute-start | bytes 122888 | tf_op jit(solution)/shard_map/ppermute | solution.py:30
  77.4 2.3 %copy-start.9 = (bf16[80,256]{1,0:T(8,128)(2,1)}, bf16[80,256]{1,0:T(8,128)(2,1)S(1)}, u32[]{:S(2)}) copy-start(bf16[80,256]{1,0:T(8,128)(2,1)S(1)} %collective-permute-done.12.refs_1_) | copy-start | bytes 122884
  81.8 1.3 %collective-permute-start.15 = (f32[1,128]{1,0:T(1,128)}, f32[1,128]{1,0:T(1,128)S(1)}, u32[]{:S(2)}, u32[]{:S(2)}) collective-permute-start(f32[1,128]{1,0:T(1,128)} %get-tuple-element.30), channel_id=1, source_target_pairs={{0,4},{4,0},{8,12},{12,8},{16,20},{20,16},{24,28},{28,24},{1,5},{5... | collective-permute-start | bytes 1544 | tf_op jit(solution)/shard_map/ppermute | solution.py:26
  83.8 3.6 %collective-permute-start.16 = (f32[1,128]{1,0:T(1,128)S(1)}, f32[1,128]{1,0:T(1,128)S(1)}, u32[]{:S(2)}, u32[]{:S(2)}) collective-permute-start(f32[1,128]{1,0:T(1,128)S(1)} %add.571), channel_id=1, source_target_pairs={{0,8},{4,12},{8,0},{12,4},{16,24},{20,28},{24,16},{28,20},{1,9},{5... | collective-permute-start | bytes 1544 | tf_op jit(solution)/shard_map/ppermute | solution.py:26
  (5 other events, 3.6 us)
